TPU v7x, 32 devices: a whole 2x2x4 slice. The times are simulated.
32 devices in a mesh: gx: 8 (over y, x, core), gy: 4 (over z).
Axes of the slice: x: 2, y: 2, z: 4, core: 2. Of those that a mesh axis runs over, the one named last changes fastest.
Arguments:
- tiles: float32 [256, 5, 128, 128], P(('gx', 'gy')), may hold values from 0 to 0.003125
- cols: int32 [256, 5], P(('gx', 'gy')), may hold values from 0 to 17, as said below
- boundary: int32 [32, 2], P(('gx', 'gy')), may hold values from 0 to 7, as said below
- current: float32 [32768, 64], P(('gx', 'gy')), may hold values from -44 to 44
- previous: float32 [32768, 64], P(('gx', 'gy')), may hold values from -44 to 44
Outputs:
- filtered: float32 [32768, 64], P(('gx', 'gy'))
- gram: float32 [64, 64], replicated
Inputs may be any that keep to these rules, and one draw needn't show every extreme that they name: `cols`: in each part, block row r has r in its first tile slot; each value from 8 up to the table's last entry occurs exactly once among the part's block rows. `boundary`: the 2 entries of a row are distinct block rows of the part.
All inputs are finite; a program needn't handle non-finite values.
Results may differ from a plain program's by a relative error of at most 0.0003.
Values sent between devices are 32-bit elements; how exact they have to be, the bound alone decides.
A program may use at most 64 MiB of HBM per device.

v0:
```python
import jax
import jax.numpy as jnp
from jax import lax
from jax.sharding import PartitionSpec as P

ITERS = 3


def partner(value, axis, stride):
    mask = 2**stride
    pairs = [(source, source ^ mask) for source in range(lax.axis_size(axis))]
    return lax.ppermute(value, axis, pairs)


def shards(tiles, cols, boundary, current, previous):
    size_x = lax.axis_size("gx")
    size_y = lax.axis_size("gy")
    block_rows = cols.shape[0]
    block_size = tiles.shape[-1]
    vectors = current.shape[1]
    bits_low = list(range(size_y.bit_length() - 1))
    bits_high = list(range(size_x.bit_length() - 1))
    field = current
    older = previous
    for step in range(ITERS):
        blocks = field.reshape(block_rows, block_size, vectors)
        outgoing = jnp.take(blocks, boundary[0], axis=0)

        def from_low():
            return [partner(outgoing, "gy", which_bit) for which_bit in bits_low]

        def from_high():
            return [partner(outgoing, "gx", which_bit) for which_bit in bits_high]

        low_ghosts = from_low()
        high_ghosts = from_high()
        table = jnp.concatenate([blocks] + low_ghosts + high_ghosts, axis=0)
        operands = jnp.take(table, cols, axis=0)
        product = jnp.einsum("rtij,rtjv->riv", tiles, operands, precision=lax.Precision.HIGHEST)
        product = product.reshape(block_rows * block_size, vectors)
        nexter = 2.0 / 0.75 * (product - 0.25 * field) - older
        older = field
        field = nexter
    partial_gram = jnp.dot(
        field.T, field, precision=lax.Precision.HIGHEST, preferred_element_type=jnp.float32
    )
    total_rows = block_rows * block_size * size_x * size_y
    gram = lax.psum(partial_gram, ("gx", "gy")) / float(total_rows)
    return (field, gram)


def solution(mesh):
    in_specs = (
        P(("gx", "gy"), None, None, None),
        P(("gx", "gy"), None),
        P(("gx", "gy"), None),
        P(("gx", "gy"), None),
        P(("gx", "gy"), None),
    )
    out_specs = (P(("gx", "gy"), None), P())
    return jax.shard_map(shards, mesh=mesh, in_specs=in_specs, out_specs=out_specs, check_vma=False)
```

profile of v0, /device:TPU:0, one launch (start us, length us, event | category | flops | bytes accessed | tf_op | source)
XLA Modules:
  0.0 96.7 jit_solution(13172485153724881354)
XLA Ops:
  0.6 0.8 compare_and_fusion.1
  1.5 0.7 compare_select_fusion.1
  2.1 1.0 copy_bitcast_fusion.2
  3.7 3.0 %collective-permute-start.4 = (f32[2,128,64]{1,2,0:T(8,128)S(1)}, f32[2,128,64]{1,2,0:T(8,128)S(1)}, u32[]{:S(2)}, u32[]{:S(2)}) collective-permute-start(f32[2,128,64]{1,2,0:T(8,128)S(1)} %broadcast_select_fusion.2), channel_id=1, source_target_pairs={{0,16},{4,20},{8,24},{12,28},{16,0},{20,4},{24,8},{28,12},{1,17},{... | collective-permute-start | bytes 196616 | tf_op jit(solution)/shard_map/ppermute | solution.py:12
  6.7 1.5 %collective-permute-start.3 = (f32[2,128,64]{1,2,0:T(8,128)S(1)}, f32[2,128,64]{1,2,0:T(8,128)S(1)}, u32[]{:S(2)}, u32[]{:S(2)}) collective-permute-start(f32[2,128,64]{1,2,0:T(8,128)S(1)} %broadcast_select_fusion.2), channel_id=1, source_target_pairs={{0,8},{4,12},{8,0},{12,4},{16,24},{20,28},{24,16},{28,20},{1,9},{5... | collective-permute-start | bytes 196616 | tf_op jit(solution)/shard_map/ppermute | solution.py:12
  8.2 2.6 %collective-permute-start.1 = (f32[2,128,64]{1,2,0:T(8,128)S(1)}, f32[2,128,64]{1,2,0:T(8,128)S(1)}, u32[]{:S(2)}, u32[]{:S(2)}) collective-permute-start(f32[2,128,64]{1,2,0:T(8,128)S(1)} %broadcast_select_fusion.2), channel_id=1, source_target_pairs={{0,2},{1,3},{2,0},{3,1},{4,6},{5,7},{6,4},{7,5},{8,10},{9,11},{10,... | collective-permute-start | bytes 196616 | tf_op jit(solution)/shard_map/ppermute | solution.py:12
  10.8 1.6 %collective-permute-start = (f32[2,128,64]{1,2,0:T(8,128)S(1)}, f32[2,128,64]{1,2,0:T(8,128)}, u32[]{:S(2)}, u32[]{:S(2)}) collective-permute-start(f32[2,128,64]{1,2,0:T(8,128)S(1)} %broadcast_select_fusion.2), channel_id=1, source_target_pairs={{0,1},{1,0},{2,3},{3,2},{4,5},{5,4},{6,7},{7,6},{8,9},{9,8},{10,11... | collective-permute-start | bytes 196616 | tf_op jit(solution)/shard_map/ppermute | solution.py:12
  12.4 0.7 compare_and_fusion
  13.1 0.7 compare_select_fusion
  13.8 1.0 constant_dynamic-update-slice_fusion.5
  15.3 0.7 pad_clamp_fusion
  16.0 0.8 constant_dynamic-update-slice_fusion.4
  16.9 1.7 %gather_fusion.1 = f32[40,128,64]{1,2,0:T(8,128)} fusion(f32[18,128,64]{1,2,0:T(8,128)S(1)} %constant_dynamic-update-slice_fusion, s32[1024]{0:T(1024)S(1)} %pad_clamp_fusion), kind=kCustom, calls=%fused_computation.1.clone | custom fusion | bytes 2621600 | tf_op jit(solution)/shard_map/jit(_take)/gather | solution.py:38
  18.6 4.7 %fusion.6 = f32[8,8,8,128]{3,2,1,0:T(8,128)S(1)} fusion(f32[8,5,128,128]{3,2,1,0:T(8,128)S(1)} %copy-done, f32[8,5,128,64]{2,3,1,0:T(8,128)} %bitcast.85, pred[8,5]{1,0:T(8,128)(4,1)S(1)} %compare_and_fusion), kind=kOutput, calls=%fused_computation.12 | convolution fusion | flops 503644160 | bytes 4194344 | tf_op jit(solution)/shard_map/rtij,rtjv->riv/dot_general | solution.py:39
  23.4 0.7 copy-done.2
  25.8 0.8 collective-permute-start.6
  26.6 1.5 %collective-permute-start.5 = (f32[2,128,64]{1,2,0:T(8,128)S(1)}, f32[2,128,64]{1,2,0:T(8,128)S(1)}, u32[]{:S(2)}, u32[]{:S(2)}) collective-permute-start(f32[2,128,64]{1,2,0:T(8,128)S(1)} %broadcast_select_fusion.1), channel_id=1, source_target_pairs={{0,1},{1,0},{2,3},{3,2},{4,5},{5,4},{6,7},{7,6},{8,9},{9,8},{10,11... | collective-permute-start | bytes 196616 | tf_op jit(solution)/shard_map/ppermute | solution.py:12
  28.1 1.1 %constant_dynamic-update-slice_fusion.11 = f32[18,128,64]{1,2,0:T(8,128)S(1)} fusion(f32[1024,64]{0,1:T(8,128)} %param.13, f32[1024,64]{0,1:T(8,128)S(1)} %copy-done.1, f32[8,8,8,128]{3,2,1,0:T(8,128)} %copy-done.2), kind=kLoop, calls=%fused_computation.45 | loop fusion | flops 262143 | bytes 1048576
  29.1 2.0 %collective-permute-done.5 = f32[2,128,64]{1,2,0:T(8,128)S(1)} collective-permute-done((f32[2,128,64]{1,2,0:T(8,128)S(1)}, f32[2,128,64]{1,2,0:T(8,128)S(1)}, u32[]{:S(2)}, u32[]{:S(2)}) %collective-permute-start.5) | collective-permute-done | bytes 65568 | tf_op jit(solution)/shard_map/ppermute | solution.py:12
  31.2 1.4 %collective-permute-done.6 = f32[2,128,64]{1,2,0:T(8,128)S(1)} collective-permute-done((f32[2,128,64]{1,2,0:T(8,128)S(1)}, f32[2,128,64]{1,2,0:T(8,128)S(1)}, u32[]{:S(2)}, u32[]{:S(2)}) %collective-permute-start.6) | collective-permute-done | bytes 65568 | tf_op jit(solution)/shard_map/ppermute | solution.py:12
  32.7 1.7 %gather_fusion.3 = f32[40,128,64]{1,2,0:T(8,128)} fusion(f32[18,128,64]{1,2,0:T(8,128)S(1)} %constant_dynamic-update-slice_fusion.6, s32[1024]{0:T(1024)S(1)} %pad_clamp_fusion), kind=kCustom, calls=%fused_computation.4.clone | custom fusion | bytes 2621600 | tf_op jit(solution)/shard_map/jit(_take)/gather | solution.py:38
  34.4 4.8 %fusion.9 = f32[8,8,8,128]{3,2,1,0:T(8,128)S(1)} fusion(f32[8,5,128,128]{3,2,1,0:T(8,128)S(1)} %copy-done, f32[8,5,128,64]{2,3,1,0:T(8,128)} %bitcast.86, pred[8,5]{1,0:T(8,128)(4,1)S(1)} %compare_and_fusion), kind=kOutput, calls=%fused_computation.13 | convolution fusion | flops 503644160 | bytes 4194344 | tf_op jit(solution)/shard_map/rtij,rtjv->riv/dot_general | solution.py:39
  39.9 0.7 copy-done.10
  41.2 1.5 %collective-permute-start.14 = (f32[2,128,64]{1,2,0:T(8,128)S(1)}, f32[2,128,64]{1,2,0:T(8,128)S(1)}, u32[]{:S(2)}, u32[]{:S(2)}) collective-permute-start(f32[2,128,64]{1,2,0:T(8,128)S(1)} %broadcast_select_fusion), channel_id=1, source_target_pairs={{0,16},{4,20},{8,24},{12,28},{16,0},{20,4},{24,8},{28,12},{1,17},{... | collective-permute-start | bytes 196616 | tf_op jit(solution)/shard_map/ppermute | solution.py:12
  42.8 1.5 %collective-permute-start.13 = (f32[2,128,64]{1,2,0:T(8,128)S(1)}, f32[2,128,64]{1,2,0:T(8,128)S(1)}, u32[]{:S(2)}, u32[]{:S(2)}) collective-permute-start(f32[2,128,64]{1,2,0:T(8,128)S(1)} %broadcast_select_fusion), channel_id=1, source_target_pairs={{0,8},{4,12},{8,0},{12,4},{16,24},{20,28},{24,16},{28,20},{1,9},{5... | collective-permute-start | bytes 196616 | tf_op jit(solution)/shard_map/ppermute | solution.py:12
  44.3 0.9 collective-permute-start.11
  45.2 1.7 %collective-permute-start.10 = (f32[2,128,64]{1,2,0:T(8,128)S(1)}, f32[2,128,64]{1,2,0:T(8,128)S(1)}, u32[]{:S(2)}, u32[]{:S(2)}) collective-permute-start(f32[2,128,64]{1,2,0:T(8,128)S(1)} %broadcast_select_fusion), channel_id=1, source_target_pairs={{0,1},{1,0},{2,3},{3,2},{4,5},{5,4},{6,7},{7,6},{8,9},{9,8},{10,11... | collective-permute-start | bytes 196616 | tf_op jit(solution)/shard_map/ppermute | solution.py:12
  46.8 1.0 constant_dynamic-update-slice_fusion.17
  47.8 3.0 %collective-permute-done.10 = f32[2,128,64]{1,2,0:T(8,128)S(1)} collective-permute-done((f32[2,128,64]{1,2,0:T(8,128)S(1)}, f32[2,128,64]{1,2,0:T(8,128)S(1)}, u32[]{:S(2)}, u32[]{:S(2)}) %collective-permute-start.10) | collective-permute-done | bytes 65568 | tf_op jit(solution)/shard_map/ppermute | solution.py:12
  50.9 1.7 %gather_fusion.5 = f32[40,128,64]{1,2,0:T(8,128)} fusion(f32[18,128,64]{1,2,0:T(8,128)S(1)} %constant_dynamic-update-slice_fusion.12, s32[1024]{0:T(1024)S(1)} %pad_clamp_fusion), kind=kCustom, calls=%fused_computation.5.clone | custom fusion | bytes 2621600 | tf_op jit(solution)/shard_map/jit(_take)/gather | solution.py:38
  52.6 4.8 %fusion.12 = f32[8,8,8,128]{3,2,1,0:T(8,128)S(1)} fusion(f32[8,5,128,128]{3,2,1,0:T(8,128)S(1)} %copy-done, f32[8,5,128,64]{2,3,1,0:T(8,128)} %bitcast.84, pred[8,5]{1,0:T(8,128)(4,1)S(1)} %compare_and_fusion), kind=kOutput, calls=%fused_computation.14 | convolution fusion | flops 503644160 | bytes 4194344 | tf_op jit(solution)/shard_map/rtij,rtjv->riv/dot_general | solution.py:39
  57.9 38.2 %psum.7 = f32[64,64]{1,0:T(8,128)S(1)} all-reduce(f32[64,64]{1,0:T(8,128)S(1)} %fusion.32), channel_id=1, replica_groups=mesh['gx'=8,'gy'=4] {'gx','gy'}, use_global_device_ids=true, to_apply=%region_0.3 | all-reduce | flops 4096 | bytes 32768 | tf_op jit(solution)/shard_map/psum | solution.py:48
  (67 shorter events, 5.6 us)
Async XLA Ops:
  0.6 18.0 %copy-start = (f32[8,5,128,128]{3,2,1,0:T(8,128)S(1)}, f32[8,5,128,128]{3,2,1,0:T(8,128)}, u32[]{:S(2)}) copy-start(f32[8,5,128,128]{3,2,1,0:T(8,128)} %param.9) | copy-start | bytes 7864324
  3.7 13.2 %collective-permute-start.4 = (f32[2,128,64]{1,2,0:T(8,128)S(1)}, f32[2,128,64]{1,2,0:T(8,128)S(1)}, u32[]{:S(2)}, u32[]{:S(2)}) collective-permute-start(f32[2,128,64]{1,2,0:T(8,128)S(1)} %broadcast_select_fusion.2), channel_id=1, source_target_pairs={{0,16},{4,20},{8,24},{12,28},{16,0},{20,4},{24,8},{28,12},{1,17},{... | collective-permute-start | bytes 196616 | tf_op jit(solution)/shard_map/ppermute | solution.py:12
  6.7 10.2 %collective-permute-start.3 = (f32[2,128,64]{1,2,0:T(8,128)S(1)}, f32[2,128,64]{1,2,0:T(8,128)S(1)}, u32[]{:S(2)}, u32[]{:S(2)}) collective-permute-start(f32[2,128,64]{1,2,0:T(8,128)S(1)} %broadcast_select_fusion.2), channel_id=1, source_target_pairs={{0,8},{4,12},{8,0},{12,4},{16,24},{20,28},{24,16},{28,20},{1,9},{5... | collective-permute-start | bytes 196616 | tf_op jit(solution)/shard_map/ppermute | solution.py:12
  8.2 8.6 %collective-permute-start.2 = (f32[2,128,64]{1,2,0:T(8,128)S(1)}, f32[2,128,64]{1,2,0:T(8,128)S(1)}, u32[]{:S(2)}, u32[]{:S(2)}) collective-permute-start(f32[2,128,64]{1,2,0:T(8,128)S(1)} %broadcast_select_fusion.2), channel_id=1, source_target_pairs={{0,4},{4,0},{8,12},{12,8},{16,20},{20,16},{24,28},{28,24},{1,5},{5... | collective-permute-start | bytes 196616 | tf_op jit(solution)/shard_map/ppermute | solution.py:12
  8.2 8.6 %collective-permute-start.1 = (f32[2,128,64]{1,2,0:T(8,128)S(1)}, f32[2,128,64]{1,2,0:T(8,128)S(1)}, u32[]{:S(2)}, u32[]{:S(2)}) collective-permute-start(f32[2,128,64]{1,2,0:T(8,128)S(1)} %broadcast_select_fusion.2), channel_id=1, source_target_pairs={{0,2},{1,3},{2,0},{3,1},{4,6},{5,7},{6,4},{7,5},{8,10},{9,11},{10,... | collective-permute-start | bytes 196616 | tf_op jit(solution)/shard_map/ppermute | solution.py:12
  10.8 5.2 %collective-permute-start = (f32[2,128,64]{1,2,0:T(8,128)S(1)}, f32[2,128,64]{1,2,0:T(8,128)}, u32[]{:S(2)}, u32[]{:S(2)}) collective-permute-start(f32[2,128,64]{1,2,0:T(8,128)S(1)} %broadcast_select_fusion.2), channel_id=1, source_target_pairs={{0,1},{1,0},{2,3},{3,2},{4,5},{5,4},{6,7},{7,6},{8,9},{9,8},{10,11... | collective-permute-start | bytes 196616 | tf_op jit(solution)/shard_map/ppermute | solution.py:12
  18.6 5.5 %copy-start.1 = (f32[1024,64]{0,1:T(8,128)S(1)}, f32[1024,64]{0,1:T(8,128)}, u32[]{:S(2)}) copy-start(f32[1024,64]{0,1:T(8,128)} %param.12) | copy-start | bytes 786436
  18.6 5.5 %copy-start.5 = (f32[1024,64]{0,1:T(8,128)S(1)}, f32[1024,64]{0,1:T(8,128)}, u32[]{:S(2)}) copy-start(f32[1024,64]{0,1:T(8,128)} %param.13) | copy-start | bytes 786436
  23.4 0.7 copy-start.2
  24.8 7.9 %collective-permute-start.9 = (f32[2,128,64]{1,2,0:T(8,128)S(1)}, f32[2,128,64]{1,2,0:T(8,128)S(1)}, u32[]{:S(2)}, u32[]{:S(2)}) collective-permute-start(f32[2,128,64]{1,2,0:T(8,128)S(1)} %broadcast_select_fusion.1), channel_id=1, source_target_pairs={{0,16},{4,20},{8,24},{12,28},{16,0},{20,4},{24,8},{28,12},{1,17},{... | collective-permute-start | bytes 196616 | tf_op jit(solution)/shard_map/ppermute | solution.py:12
  25.3 7.4 %collective-permute-start.8 = (f32[2,128,64]{1,2,0:T(8,128)S(1)}, f32[2,128,64]{1,2,0:T(8,128)S(1)}, u32[]{:S(2)}, u32[]{:S(2)}) collective-permute-start(f32[2,128,64]{1,2,0:T(8,128)S(1)} %broadcast_select_fusion.1), channel_id=1, source_target_pairs={{0,8},{4,12},{8,0},{12,4},{16,24},{20,28},{24,16},{28,20},{1,9},{5... | collective-permute-start | bytes 196616 | tf_op jit(solution)/shard_map/ppermute | solution.py:12
  25.8 6.8 %collective-permute-start.7 = (f32[2,128,64]{1,2,0:T(8,128)S(1)}, f32[2,128,64]{1,2,0:T(8,128)S(1)}, u32[]{:S(2)}, u32[]{:S(2)}) collective-permute-start(f32[2,128,64]{1,2,0:T(8,128)S(1)} %broadcast_select_fusion.1), channel_id=1, source_target_pairs={{0,4},{4,0},{8,12},{12,8},{16,20},{20,16},{24,28},{28,24},{1,5},{5... | collective-permute-start | bytes 196616 | tf_op jit(solution)/shard_map/ppermute | solution.py:12
  25.8 6.8 %collective-permute-start.6 = (f32[2,128,64]{1,2,0:T(8,128)S(1)}, f32[2,128,64]{1,2,0:T(8,128)S(1)}, u32[]{:S(2)}, u32[]{:S(2)}) collective-permute-start(f32[2,128,64]{1,2,0:T(8,128)S(1)} %broadcast_select_fusion.1), channel_id=1, source_target_pairs={{0,2},{1,3},{2,0},{3,1},{4,6},{5,7},{6,4},{7,5},{8,10},{9,11},{10,... | collective-permute-start | bytes 196616 | tf_op jit(solution)/shard_map/ppermute | solution.py:12
  26.6 4.6 %collective-permute-start.5 = (f32[2,128,64]{1,2,0:T(8,128)S(1)}, f32[2,128,64]{1,2,0:T(8,128)S(1)}, u32[]{:S(2)}, u32[]{:S(2)}) collective-permute-start(f32[2,128,64]{1,2,0:T(8,128)S(1)} %broadcast_select_fusion.1), channel_id=1, source_target_pairs={{0,1},{1,0},{2,3},{3,2},{4,5},{5,4},{6,7},{7,6},{8,9},{9,8},{10,11... | collective-permute-start | bytes 196616 | tf_op jit(solution)/shard_map/ppermute | solution.py:12
  34.4 4.8 %copy-start.3 = (f32[8,8,8,128]{3,2,1,0:T(8,128)S(1)}, f32[8,8,8,128]{3,2,1,0:T(8,128)}, u32[]{:S(2)}) copy-start(f32[8,8,8,128]{3,2,1,0:T(8,128)} %copy-done.2) | copy-start | bytes 786436
  34.4 4.8 %copy-start.6 = (f32[1024,64]{0,1:T(8,128)S(1)}, f32[1024,64]{0,1:T(8,128)}, u32[]{:S(2)}) copy-start(f32[1024,64]{0,1:T(8,128)} %param.13) | copy-start | bytes 786436
  39.2 0.7 copy-start.8
  39.9 0.7 copy-start.10
  41.2 9.6 %collective-permute-start.14 = (f32[2,128,64]{1,2,0:T(8,128)S(1)}, f32[2,128,64]{1,2,0:T(8,128)S(1)}, u32[]{:S(2)}, u32[]{:S(2)}) collective-permute-start(f32[2,128,64]{1,2,0:T(8,128)S(1)} %broadcast_select_fusion), channel_id=1, source_target_pairs={{0,16},{4,20},{8,24},{12,28},{16,0},{20,4},{24,8},{28,12},{1,17},{... | collective-permute-start | bytes 196616 | tf_op jit(solution)/shard_map/ppermute | solution.py:12
  42.8 8.1 %collective-permute-start.13 = (f32[2,128,64]{1,2,0:T(8,128)S(1)}, f32[2,128,64]{1,2,0:T(8,128)S(1)}, u32[]{:S(2)}, u32[]{:S(2)}) collective-permute-start(f32[2,128,64]{1,2,0:T(8,128)S(1)} %broadcast_select_fusion), channel_id=1, source_target_pairs={{0,8},{4,12},{8,0},{12,4},{16,24},{20,28},{24,16},{28,20},{1,9},{5... | collective-permute-start | bytes 196616 | tf_op jit(solution)/shard_map/ppermute | solution.py:12
  44.3 6.6 %collective-permute-start.12 = (f32[2,128,64]{1,2,0:T(8,128)S(1)}, f32[2,128,64]{1,2,0:T(8,128)S(1)}, u32[]{:S(2)}, u32[]{:S(2)}) collective-permute-start(f32[2,128,64]{1,2,0:T(8,128)S(1)} %broadcast_select_fusion), channel_id=1, source_target_pairs={{0,4},{4,0},{8,12},{12,8},{16,20},{20,16},{24,28},{28,24},{1,5},{5... | collective-permute-start | bytes 196616 | tf_op jit(solution)/shard_map/ppermute | solution.py:12
  44.3 6.5 %collective-permute-start.11 = (f32[2,128,64]{1,2,0:T(8,128)S(1)}, f32[2,128,64]{1,2,0:T(8,128)S(1)}, u32[]{:S(2)}, u32[]{:S(2)}) collective-permute-start(f32[2,128,64]{1,2,0:T(8,128)S(1)} %broadcast_select_fusion), channel_id=1, source_target_pairs={{0,2},{1,3},{2,0},{3,1},{4,6},{5,7},{6,4},{7,5},{8,10},{9,11},{10,... | collective-permute-start | bytes 196616 | tf_op jit(solution)/shard_map/ppermute | solution.py:12
  45.2 5.6 %collective-permute-start.10 = (f32[2,128,64]{1,2,0:T(8,128)S(1)}, f32[2,128,64]{1,2,0:T(8,128)S(1)}, u32[]{:S(2)}, u32[]{:S(2)}) collective-permute-start(f32[2,128,64]{1,2,0:T(8,128)S(1)} %broadcast_select_fusion), channel_id=1, source_target_pairs={{0,1},{1,0},{2,3},{3,2},{4,5},{5,4},{6,7},{7,6},{8,9},{9,8},{10,11... | collective-permute-start | bytes 196616 | tf_op jit(solution)/shard_map/ppermute | solution.py:12
  52.6 4.8 %copy-start.4 = (f32[8,8,8,128]{3,2,1,0:T(8,128)S(1)}, f32[8,8,8,128]{3,2,1,0:T(8,128)}, u32[]{:S(2)}) copy-start(f32[8,8,8,128]{3,2,1,0:T(8,128)} %copy-done.2) | copy-start | bytes 786436
  52.6 4.8 %copy-start.7 = (f32[1024,64]{0,1:T(8,128)S(1)}, f32[1024,64]{0,1:T(8,128)}, u32[]{:S(2)}) copy-start(f32[1024,64]{0,1:T(8,128)} %param.13) | copy-start | bytes 786436
  52.6 4.8 %copy-start.9 = (f32[8,8,8,128]{3,2,1,0:T(8,128)S(1)}, f32[8,8,8,128]{3,2,1,0:T(8,128)}, u32[]{:S(2)}) copy-start(f32[8,8,8,128]{3,2,1,0:T(8,128)} %copy-done.8) | copy-start | bytes 786436
  57.5 39.2 %copy-start.11 = (f32[1024,64]{0,1:T(8,128)}, f32[1024,64]{0,1:T(8,128)S(1)}, u32[]{:S(2)}) copy-start(f32[1024,64]{0,1:T(8,128)S(1)} %fusion.22) | copy-start | bytes 786436
where the time goes:
time: 97.2 us; the launch traced here: 96.7 us
  blocking collectives  38.2 us (39%)
  starting transfers between devices  17.5 us (18%)
  matrix products  14.6 us (15%)
  local copies, waits for them, and re-layouts  13.2 us (14%)
  waiting for transfers between devices  6.51 us (7%)
  other arithmetic  5.71 us (6%)
    psum x1, blocking collectives, shards(): gram = lax.psum(partial_gram, ('gx', 'gy')) / float(total_rows)  38.2 us
    ppermute x15, starting transfers between devices, partner(): return lax.ppermute(value, axis, pairs)  17.5 us
    dot_general x3, matrix products, shards(): jnp.einsum('rtij,rtjv->riv', tiles, operands, precision=lax.Precision.HIG...  14.3 us
    ppermute x15, waiting for transfers between devices, partner(): return lax.ppermute(value, axis, pairs)  6.51 us
    gather x3, local copies, waits for them, and re-layouts, shards(): operands = jnp.take(table, cols, axis=0)  5.09 us
    unnamed x38, local copies, waits for them, and re-layouts  4.88 us
  transfers between devices with their start and end apart: 15, of which 3 were waited for; matrix products, arithmetic and copies ran while one was open for 7% of the time, Pallas kernels for 0%

commit v1 on v0

--- a/solution.py
+++ b/solution.py
@@ -4,6 +4,10 @@
 from jax.sharding import PartitionSpec as P
 
 ITERS = 3
+
+
+def wrap_pages(piece_in):
+    return jnp.sum(lax.all_gather(piece_in, ("gx", "gy")), axis=0)
 
 
 def partner(value, axis, stride):
@@ -45,7 +49,7 @@
         field.T, field, precision=lax.Precision.HIGHEST, preferred_element_type=jnp.float32
     )
     total_rows = block_rows * block_size * size_x * size_y
-    gram = lax.psum(partial_gram, ("gx", "gy")) / float(total_rows)
+    gram = wrap_pages(partial_gram) / float(total_rows)
     return (field, gram)
 
 

time: 97.2 us -> 140 us (1.44)
  blocking collectives: 38.2 us -> 79.6 us
    all_gather x0 -> x1, blocking collectives: none -> 79.6 us  [wrap_pages(): return jnp.sum(lax.all_gather(piece_in, ('gx', 'gy')), axis=0)]
    psum x1 -> x0, blocking collectives: 38.2 us -> none  [shards(): gram = lax.psum(partial_gram, ('gx', 'gy')) / float(total_rows)]
  transfers between devices with their start and end apart: 15 -> 15, of which waited for: 3 -> 3; matrix products, arithmetic and copies ran while one was open for 7% -> 5% of each run, Pallas kernels for 0% -> 0%
where the time goes in v1:
time: 140 us; the launch traced here: 139 us
  blocking collectives  79.6 us (57%)
  starting transfers between devices  17.5 us (12%)
  matrix products  14.6 us (10%)
  local copies, waits for them, and re-layouts  13.2 us (9%)
  other arithmetic  7.03 us (5%)
  waiting for transfers between devices  6.51 us (5%)
    all_gather x1, blocking collectives, wrap_pages(): return jnp.sum(lax.all_gather(piece_in, ('gx', 'gy')), axis=0)  79.6 us
    ppermute x15, starting transfers between devices, partner(): return lax.ppermute(value, axis, pairs)  17.5 us
    dot_general x3, matrix products, shards(): jnp.einsum('rtij,rtjv->riv', tiles, operands, precision=lax.Precision.HIG...  14.3 us
    ppermute x15, waiting for transfers between devices, partner(): return lax.ppermute(value, axis, pairs)  6.51 us
    gather x3, local copies, waits for them, and re-layouts, shards(): operands = jnp.take(table, cols, axis=0)  5.09 us
    unnamed x38, local copies, waits for them, and re-layouts  4.88 us
  transfers between devices with their start and end apart: 15, of which 3 were waited for; matrix products, arithmetic and copies ran while one was open for 5% of the time, Pallas kernels for 0%

profile of v1, /device:TPU:0, one launch (start us, length us, event | category | flops | bytes accessed | tf_op | source)
XLA Modules:
  0.0 139.5 jit_solution(4179518517871306786)
XLA Ops:
  0.6 0.8 compare_and_fusion.1
  2.1 1.0 copy_bitcast_fusion.2
  3.7 3.0 %collective-permute-start.4 = (f32[2,128,64]{1,2,0:T(8,128)S(1)}, f32[2,128,64]{1,2,0:T(8,128)S(1)}, u32[]{:S(2)}, u32[]{:S(2)}) collective-permute-start(f32[2,128,64]{1,2,0:T(8,128)S(1)} %broadcast_select_fusion.2), channel_id=1, source_target_pairs={{0,16},{4,20},{8,24},{12,28},{16,0},{20,4},{24,8},{28,12},{1,17},{... | collective-permute-start | bytes 196616 | tf_op jit(solution)/shard_map/ppermute | solution.py:16
  6.7 1.5 %collective-permute-start.3 = (f32[2,128,64]{1,2,0:T(8,128)S(1)}, f32[2,128,64]{1,2,0:T(8,128)S(1)}, u32[]{:S(2)}, u32[]{:S(2)}) collective-permute-start(f32[2,128,64]{1,2,0:T(8,128)S(1)} %broadcast_select_fusion.2), channel_id=1, source_target_pairs={{0,8},{4,12},{8,0},{12,4},{16,24},{20,28},{24,16},{28,20},{1,9},{5... | collective-permute-start | bytes 196616 | tf_op jit(solution)/shard_map/ppermute | solution.py:16
  8.2 2.6 %collective-permute-start.1 = (f32[2,128,64]{1,2,0:T(8,128)S(1)}, f32[2,128,64]{1,2,0:T(8,128)S(1)}, u32[]{:S(2)}, u32[]{:S(2)}) collective-permute-start(f32[2,128,64]{1,2,0:T(8,128)S(1)} %broadcast_select_fusion.2), channel_id=1, source_target_pairs={{0,2},{1,3},{2,0},{3,1},{4,6},{5,7},{6,4},{7,5},{8,10},{9,11},{10,... | collective-permute-start | bytes 196616 | tf_op jit(solution)/shard_map/ppermute | solution.py:16
  10.8 1.6 %collective-permute-start = (f32[2,128,64]{1,2,0:T(8,128)S(1)}, f32[2,128,64]{1,2,0:T(8,128)}, u32[]{:S(2)}, u32[]{:S(2)}) collective-permute-start(f32[2,128,64]{1,2,0:T(8,128)S(1)} %broadcast_select_fusion.2), channel_id=1, source_target_pairs={{0,1},{1,0},{2,3},{3,2},{4,5},{5,4},{6,7},{7,6},{8,9},{9,8},{10,11... | collective-permute-start | bytes 196616 | tf_op jit(solution)/shard_map/ppermute | solution.py:16
  12.4 0.7 compare_and_fusion
  13.1 0.7 compare_select_fusion
  13.8 1.0 constant_dynamic-update-slice_fusion.5
  15.3 0.7 pad_clamp_fusion
  16.0 0.8 constant_dynamic-update-slice_fusion.4
  16.9 1.7 %gather_fusion.1 = f32[40,128,64]{1,2,0:T(8,128)} fusion(f32[18,128,64]{1,2,0:T(8,128)S(1)} %constant_dynamic-update-slice_fusion, s32[1024]{0:T(1024)S(1)} %pad_clamp_fusion), kind=kCustom, calls=%fused_computation.1.clone | custom fusion | bytes 2621600 | tf_op jit(solution)/shard_map/jit(_take)/gather | solution.py:42
  18.6 4.7 %fusion.6 = f32[8,8,8,128]{3,2,1,0:T(8,128)S(1)} fusion(f32[8,5,128,128]{3,2,1,0:T(8,128)S(1)} %copy-done, f32[8,5,128,64]{2,3,1,0:T(8,128)} %bitcast.86, pred[8,5]{1,0:T(8,128)(4,1)S(1)} %compare_and_fusion), kind=kOutput, calls=%fused_computation.12 | convolution fusion | flops 503644160 | bytes 4194344 | tf_op jit(solution)/shard_map/rtij,rtjv->riv/dot_general | solution.py:43
  23.4 0.7 copy-done.2
  25.8 0.8 collective-permute-start.6
  26.6 1.5 %collective-permute-start.5 = (f32[2,128,64]{1,2,0:T(8,128)S(1)}, f32[2,128,64]{1,2,0:T(8,128)S(1)}, u32[]{:S(2)}, u32[]{:S(2)}) collective-permute-start(f32[2,128,64]{1,2,0:T(8,128)S(1)} %broadcast_select_fusion.1), channel_id=1, source_target_pairs={{0,1},{1,0},{2,3},{3,2},{4,5},{5,4},{6,7},{7,6},{8,9},{9,8},{10,11... | collective-permute-start | bytes 196616 | tf_op jit(solution)/shard_map/ppermute | solution.py:16
  28.1 1.1 constant_dynamic-update-slice_fusion.11
  29.1 2.0 %collective-permute-done.5 = f32[2,128,64]{1,2,0:T(8,128)S(1)} collective-permute-done((f32[2,128,64]{1,2,0:T(8,128)S(1)}, f32[2,128,64]{1,2,0:T(8,128)S(1)}, u32[]{:S(2)}, u32[]{:S(2)}) %collective-permute-start.5) | collective-permute-done | bytes 65568 | tf_op jit(solution)/shard_map/ppermute | solution.py:16
  31.2 1.4 %collective-permute-done.6 = f32[2,128,64]{1,2,0:T(8,128)S(1)} collective-permute-done((f32[2,128,64]{1,2,0:T(8,128)S(1)}, f32[2,128,64]{1,2,0:T(8,128)S(1)}, u32[]{:S(2)}, u32[]{:S(2)}) %collective-permute-start.6) | collective-permute-done | bytes 65568 | tf_op jit(solution)/shard_map/ppermute | solution.py:16
  32.7 1.7 %gather_fusion.3 = f32[40,128,64]{1,2,0:T(8,128)} fusion(f32[18,128,64]{1,2,0:T(8,128)S(1)} %constant_dynamic-update-slice_fusion.6, s32[1024]{0:T(1024)S(1)} %pad_clamp_fusion), kind=kCustom, calls=%fused_computation.4.clone | custom fusion | bytes 2621600 | tf_op jit(solution)/shard_map/jit(_take)/gather | solution.py:42
  34.4 4.8 %fusion.9 = f32[8,8,8,128]{3,2,1,0:T(8,128)S(1)} fusion(f32[8,5,128,128]{3,2,1,0:T(8,128)S(1)} %copy-done, f32[8,5,128,64]{2,3,1,0:T(8,128)} %bitcast.87, pred[8,5]{1,0:T(8,128)(4,1)S(1)} %compare_and_fusion), kind=kOutput, calls=%fused_computation.13 | convolution fusion | flops 503644160 | bytes 4194344 | tf_op jit(solution)/shard_map/rtij,rtjv->riv/dot_general | solution.py:43
  39.9 0.7 copy-done.10
  41.2 1.5 %collective-permute-start.14 = (f32[2,128,64]{1,2,0:T(8,128)S(1)}, f32[2,128,64]{1,2,0:T(8,128)S(1)}, u32[]{:S(2)}, u32[]{:S(2)}) collective-permute-start(f32[2,128,64]{1,2,0:T(8,128)S(1)} %broadcast_select_fusion), channel_id=1, source_target_pairs={{0,16},{4,20},{8,24},{12,28},{16,0},{20,4},{24,8},{28,12},{1,17},{... | collective-permute-start | bytes 196616 | tf_op jit(solution)/shard_map/ppermute | solution.py:16
  42.8 1.5 %collective-permute-start.13 = (f32[2,128,64]{1,2,0:T(8,128)S(1)}, f32[2,128,64]{1,2,0:T(8,128)S(1)}, u32[]{:S(2)}, u32[]{:S(2)}) collective-permute-start(f32[2,128,64]{1,2,0:T(8,128)S(1)} %broadcast_select_fusion), channel_id=1, source_target_pairs={{0,8},{4,12},{8,0},{12,4},{16,24},{20,28},{24,16},{28,20},{1,9},{5... | collective-permute-start | bytes 196616 | tf_op jit(solution)/shard_map/ppermute | solution.py:16
  44.3 0.9 collective-permute-start.11
  45.2 1.7 %collective-permute-start.10 = (f32[2,128,64]{1,2,0:T(8,128)S(1)}, f32[2,128,64]{1,2,0:T(8,128)S(1)}, u32[]{:S(2)}, u32[]{:S(2)}) collective-permute-start(f32[2,128,64]{1,2,0:T(8,128)S(1)} %broadcast_select_fusion), channel_id=1, source_target_pairs={{0,1},{1,0},{2,3},{3,2},{4,5},{5,4},{6,7},{7,6},{8,9},{9,8},{10,11... | collective-permute-start | bytes 196616 | tf_op jit(solution)/shard_map/ppermute | solution.py:16
  46.8 1.0 constant_dynamic-update-slice_fusion.17
  47.8 3.0 %collective-permute-done.10 = f32[2,128,64]{1,2,0:T(8,128)S(1)} collective-permute-done((f32[2,128,64]{1,2,0:T(8,128)S(1)}, f32[2,128,64]{1,2,0:T(8,128)S(1)}, u32[]{:S(2)}, u32[]{:S(2)}) %collective-permute-start.10) | collective-permute-done | bytes 65568 | tf_op jit(solution)/shard_map/ppermute | solution.py:16
  50.9 1.7 %gather_fusion.5 = f32[40,128,64]{1,2,0:T(8,128)} fusion(f32[18,128,64]{1,2,0:T(8,128)S(1)} %constant_dynamic-update-slice_fusion.12, s32[1024]{0:T(1024)S(1)} %pad_clamp_fusion), kind=kCustom, calls=%fused_computation.5.clone | custom fusion | bytes 2621600 | tf_op jit(solution)/shard_map/jit(_take)/gather | solution.py:42
  52.6 4.8 %fusion.12 = f32[8,8,8,128]{3,2,1,0:T(8,128)S(1)} fusion(f32[8,5,128,128]{3,2,1,0:T(8,128)S(1)} %copy-done, f32[8,5,128,64]{2,3,1,0:T(8,128)} %bitcast.85, pred[8,5]{1,0:T(8,128)(4,1)S(1)} %compare_and_fusion), kind=kOutput, calls=%fused_computation.14 | convolution fusion | flops 503644160 | bytes 4194344 | tf_op jit(solution)/shard_map/rtij,rtjv->riv/dot_general | solution.py:43
  57.9 79.6 %all-gather = f32[2048,64]{1,0:T(8,128)} all-gather(f32[64,64]{1,0:T(8,128)S(1)} %fusion.32), channel_id=2, replica_groups=mesh['gx'=8,'gy'=4] {'gx','gy'}, dimensions={0}, use_global_device_ids=true | all-gather | bytes 540672 | tf_op jit(solution)/shard_map/all_gather | solution.py:10
  137.6 1.3 reduce_sum.9
  (68 shorter events, 6.2 us)
Async XLA Ops:
  0.6 18.0 %copy-start = (f32[8,5,128,128]{3,2,1,0:T(8,128)S(1)}, f32[8,5,128,128]{3,2,1,0:T(8,128)}, u32[]{:S(2)}) copy-start(f32[8,5,128,128]{3,2,1,0:T(8,128)} %param.9) | copy-start | bytes 7864324
  3.7 13.2 %collective-permute-start.4 = (f32[2,128,64]{1,2,0:T(8,128)S(1)}, f32[2,128,64]{1,2,0:T(8,128)S(1)}, u32[]{:S(2)}, u32[]{:S(2)}) collective-permute-start(f32[2,128,64]{1,2,0:T(8,128)S(1)} %broadcast_select_fusion.2), channel_id=1, source_target_pairs={{0,16},{4,20},{8,24},{12,28},{16,0},{20,4},{24,8},{28,12},{1,17},{... | collective-permute-start | bytes 196616 | tf_op jit(solution)/shard_map/ppermute | solution.py:16
  6.7 10.2 %collective-permute-start.3 = (f32[2,128,64]{1,2,0:T(8,128)S(1)}, f32[2,128,64]{1,2,0:T(8,128)S(1)}, u32[]{:S(2)}, u32[]{:S(2)}) collective-permute-start(f32[2,128,64]{1,2,0:T(8,128)S(1)} %broadcast_select_fusion.2), channel_id=1, source_target_pairs={{0,8},{4,12},{8,0},{12,4},{16,24},{20,28},{24,16},{28,20},{1,9},{5... | collective-permute-start | bytes 196616 | tf_op jit(solution)/shard_map/ppermute | solution.py:16
  8.2 8.6 %collective-permute-start.2 = (f32[2,128,64]{1,2,0:T(8,128)S(1)}, f32[2,128,64]{1,2,0:T(8,128)S(1)}, u32[]{:S(2)}, u32[]{:S(2)}) collective-permute-start(f32[2,128,64]{1,2,0:T(8,128)S(1)} %broadcast_select_fusion.2), channel_id=1, source_target_pairs={{0,4},{4,0},{8,12},{12,8},{16,20},{20,16},{24,28},{28,24},{1,5},{5... | collective-permute-start | bytes 196616 | tf_op jit(solution)/shard_map/ppermute | solution.py:16
  8.2 8.6 %collective-permute-start.1 = (f32[2,128,64]{1,2,0:T(8,128)S(1)}, f32[2,128,64]{1,2,0:T(8,128)S(1)}, u32[]{:S(2)}, u32[]{:S(2)}) collective-permute-start(f32[2,128,64]{1,2,0:T(8,128)S(1)} %broadcast_select_fusion.2), channel_id=1, source_target_pairs={{0,2},{1,3},{2,0},{3,1},{4,6},{5,7},{6,4},{7,5},{8,10},{9,11},{10,... | collective-permute-start | bytes 196616 | tf_op jit(solution)/shard_map/ppermute | solution.py:16
  10.8 5.2 %collective-permute-start = (f32[2,128,64]{1,2,0:T(8,128)S(1)}, f32[2,128,64]{1,2,0:T(8,128)}, u32[]{:S(2)}, u32[]{:S(2)}) collective-permute-start(f32[2,128,64]{1,2,0:T(8,128)S(1)} %broadcast_select_fusion.2), channel_id=1, source_target_pairs={{0,1},{1,0},{2,3},{3,2},{4,5},{5,4},{6,7},{7,6},{8,9},{9,8},{10,11... | collective-permute-start | bytes 196616 | tf_op jit(solution)/shard_map/ppermute | solution.py:16
  18.6 5.5 %copy-start.1 = (f32[1024,64]{0,1:T(8,128)S(1)}, f32[1024,64]{0,1:T(8,128)}, u32[]{:S(2)}) copy-start(f32[1024,64]{0,1:T(8,128)} %param.12) | copy-start | bytes 786436
  18.6 5.5 %copy-start.5 = (f32[1024,64]{0,1:T(8,128)S(1)}, f32[1024,64]{0,1:T(8,128)}, u32[]{:S(2)}) copy-start(f32[1024,64]{0,1:T(8,128)} %param.13) | copy-start | bytes 786436
  23.4 0.7 copy-start.2
  24.8 7.9 %collective-permute-start.9 = (f32[2,128,64]{1,2,0:T(8,128)S(1)}, f32[2,128,64]{1,2,0:T(8,128)S(1)}, u32[]{:S(2)}, u32[]{:S(2)}) collective-permute-start(f32[2,128,64]{1,2,0:T(8,128)S(1)} %broadcast_select_fusion.1), channel_id=1, source_target_pairs={{0,16},{4,20},{8,24},{12,28},{16,0},{20,4},{24,8},{28,12},{1,17},{... | collective-permute-start | bytes 196616 | tf_op jit(solution)/shard_map/ppermute | solution.py:16
  25.3 7.4 %collective-permute-start.8 = (f32[2,128,64]{1,2,0:T(8,128)S(1)}, f32[2,128,64]{1,2,0:T(8,128)S(1)}, u32[]{:S(2)}, u32[]{:S(2)}) collective-permute-start(f32[2,128,64]{1,2,0:T(8,128)S(1)} %broadcast_select_fusion.1), channel_id=1, source_target_pairs={{0,8},{4,12},{8,0},{12,4},{16,24},{20,28},{24,16},{28,20},{1,9},{5... | collective-permute-start | bytes 196616 | tf_op jit(solution)/shard_map/ppermute | solution.py:16
  25.8 6.8 %collective-permute-start.7 = (f32[2,128,64]{1,2,0:T(8,128)S(1)}, f32[2,128,64]{1,2,0:T(8,128)S(1)}, u32[]{:S(2)}, u32[]{:S(2)}) collective-permute-start(f32[2,128,64]{1,2,0:T(8,128)S(1)} %broadcast_select_fusion.1), channel_id=1, source_target_pairs={{0,4},{4,0},{8,12},{12,8},{16,20},{20,16},{24,28},{28,24},{1,5},{5... | collective-permute-start | bytes 196616 | tf_op jit(solution)/shard_map/ppermute | solution.py:16
  25.8 6.8 %collective-permute-start.6 = (f32[2,128,64]{1,2,0:T(8,128)S(1)}, f32[2,128,64]{1,2,0:T(8,128)S(1)}, u32[]{:S(2)}, u32[]{:S(2)}) collective-permute-start(f32[2,128,64]{1,2,0:T(8,128)S(1)} %broadcast_select_fusion.1), channel_id=1, source_target_pairs={{0,2},{1,3},{2,0},{3,1},{4,6},{5,7},{6,4},{7,5},{8,10},{9,11},{10,... | collective-permute-start | bytes 196616 | tf_op jit(solution)/shard_map/ppermute | solution.py:16
  26.6 4.6 %collective-permute-start.5 = (f32[2,128,64]{1,2,0:T(8,128)S(1)}, f32[2,128,64]{1,2,0:T(8,128)S(1)}, u32[]{:S(2)}, u32[]{:S(2)}) collective-permute-start(f32[2,128,64]{1,2,0:T(8,128)S(1)} %broadcast_select_fusion.1), channel_id=1, source_target_pairs={{0,1},{1,0},{2,3},{3,2},{4,5},{5,4},{6,7},{7,6},{8,9},{9,8},{10,11... | collective-permute-start | bytes 196616 | tf_op jit(solution)/shard_map/ppermute | solution.py:16
  34.4 4.8 %copy-start.3 = (f32[8,8,8,128]{3,2,1,0:T(8,128)S(1)}, f32[8,8,8,128]{3,2,1,0:T(8,128)}, u32[]{:S(2)}) copy-start(f32[8,8,8,128]{3,2,1,0:T(8,128)} %copy-done.2) | copy-start | bytes 786436
  34.4 4.8 %copy-start.6 = (f32[1024,64]{0,1:T(8,128)S(1)}, f32[1024,64]{0,1:T(8,128)}, u32[]{:S(2)}) copy-start(f32[1024,64]{0,1:T(8,128)} %param.13) | copy-start | bytes 786436
  39.2 0.7 copy-start.8
  39.9 0.7 copy-start.10
  41.2 9.6 %collective-permute-start.14 = (f32[2,128,64]{1,2,0:T(8,128)S(1)}, f32[2,128,64]{1,2,0:T(8,128)S(1)}, u32[]{:S(2)}, u32[]{:S(2)}) collective-permute-start(f32[2,128,64]{1,2,0:T(8,128)S(1)} %broadcast_select_fusion), channel_id=1, source_target_pairs={{0,16},{4,20},{8,24},{12,28},{16,0},{20,4},{24,8},{28,12},{1,17},{... | collective-permute-start | bytes 196616 | tf_op jit(solution)/shard_map/ppermute | solution.py:16
  42.8 8.1 %collective-permute-start.13 = (f32[2,128,64]{1,2,0:T(8,128)S(1)}, f32[2,128,64]{1,2,0:T(8,128)S(1)}, u32[]{:S(2)}, u32[]{:S(2)}) collective-permute-start(f32[2,128,64]{1,2,0:T(8,128)S(1)} %broadcast_select_fusion), channel_id=1, source_target_pairs={{0,8},{4,12},{8,0},{12,4},{16,24},{20,28},{24,16},{28,20},{1,9},{5... | collective-permute-start | bytes 196616 | tf_op jit(solution)/shard_map/ppermute | solution.py:16
  44.3 6.6 %collective-permute-start.12 = (f32[2,128,64]{1,2,0:T(8,128)S(1)}, f32[2,128,64]{1,2,0:T(8,128)S(1)}, u32[]{:S(2)}, u32[]{:S(2)}) collective-permute-start(f32[2,128,64]{1,2,0:T(8,128)S(1)} %broadcast_select_fusion), channel_id=1, source_target_pairs={{0,4},{4,0},{8,12},{12,8},{16,20},{20,16},{24,28},{28,24},{1,5},{5... | collective-permute-start | bytes 196616 | tf_op jit(solution)/shard_map/ppermute | solution.py:16
  44.3 6.5 %collective-permute-start.11 = (f32[2,128,64]{1,2,0:T(8,128)S(1)}, f32[2,128,64]{1,2,0:T(8,128)S(1)}, u32[]{:S(2)}, u32[]{:S(2)}) collective-permute-start(f32[2,128,64]{1,2,0:T(8,128)S(1)} %broadcast_select_fusion), channel_id=1, source_target_pairs={{0,2},{1,3},{2,0},{3,1},{4,6},{5,7},{6,4},{7,5},{8,10},{9,11},{10,... | collective-permute-start | bytes 196616 | tf_op jit(solution)/shard_map/ppermute | solution.py:16
  45.2 5.6 %collective-permute-start.10 = (f32[2,128,64]{1,2,0:T(8,128)S(1)}, f32[2,128,64]{1,2,0:T(8,128)S(1)}, u32[]{:S(2)}, u32[]{:S(2)}) collective-permute-start(f32[2,128,64]{1,2,0:T(8,128)S(1)} %broadcast_select_fusion), channel_id=1, source_target_pairs={{0,1},{1,0},{2,3},{3,2},{4,5},{5,4},{6,7},{7,6},{8,9},{9,8},{10,11... | collective-permute-start | bytes 196616 | tf_op jit(solution)/shard_map/ppermute | solution.py:16
  52.6 4.8 %copy-start.4 = (f32[8,8,8,128]{3,2,1,0:T(8,128)S(1)}, f32[8,8,8,128]{3,2,1,0:T(8,128)}, u32[]{:S(2)}) copy-start(f32[8,8,8,128]{3,2,1,0:T(8,128)} %copy-done.2) | copy-start | bytes 786436
  52.6 4.8 %copy-start.7 = (f32[1024,64]{0,1:T(8,128)S(1)}, f32[1024,64]{0,1:T(8,128)}, u32[]{:S(2)}) copy-start(f32[1024,64]{0,1:T(8,128)} %param.13) | copy-start | bytes 786436
  52.6 4.8 %copy-start.9 = (f32[8,8,8,128]{3,2,1,0:T(8,128)S(1)}, f32[8,8,8,128]{3,2,1,0:T(8,128)}, u32[]{:S(2)}) copy-start(f32[8,8,8,128]{3,2,1,0:T(8,128)} %copy-done.8) | copy-start | bytes 786436
  57.5 81.3 %copy-start.11 = (f32[1024,64]{0,1:T(8,128)}, f32[1024,64]{0,1:T(8,128)S(1)}, u32[]{:S(2)}) copy-start(f32[1024,64]{0,1:T(8,128)S(1)} %fusion.22) | copy-start | bytes 786436
